TPU v7x, 512 devices: a whole 4x8x8 slice. The times are simulated.
512 devices in a mesh: subj: 8 (over z), tr: 64 (over y, x, core).
Axes of the slice: x: 4, y: 8, z: 8, core: 2. Of those that a mesh axis runs over, the one named last changes fastest.
Arguments:
- features: bfloat16 [4096, 2048], P('tr', 'subj'), may hold values from -6 to 6
- block_orders: int32 [4, 64], replicated, may hold values from 0 to 63, each once within a row
- offsets: int32 [4, 4], replicated, may hold values from 0 to 8
- tap_gains: float32 [4, 4], replicated, may hold values from 0.2 to 1
- weights: bfloat16 [8, 2048, 1024], P('subj'), may hold values from -0.125 to 0.125
- signal: bfloat16 [8, 4096, 1024], P('subj', 'tr')
- block_owner: int32 [8, 256, 1], P('subj'), may hold values from 0 to 63; in each aligned block of 256 rows (0 to 255, 256 to 511, ..., all dimensions but the last counted through in order) at most 8 rows name the same one
Outputs:
- energy: float32 [8, 4096, 5], P('subj', 'tr')
- scores: float32 [8, 512, 5], P('subj', 'tr')
Inputs may be any that keep to these rules, and one draw needn't show every extreme that they name: `block_orders`: each row names every 4096 block once. `block_owner`: no owner is named by more than 8 voxel blocks of one subject.
All inputs are finite; a program needn't handle non-finite values.
Results may differ from a plain program's by a relative error of at most 0.0003.
Values may be sent and summed in bfloat16 or wider, within the bound.
A program may use at most 64 MiB of HBM per device.

v0:
```python
import jax
import jax.numpy as jnp
from jax import lax
from jax.sharding import PartitionSpec as P

MAXLAG = 8
VB = 4
CAP = 8


epsilon = 1e-06


def passed_along(value, axis, steps):
    count = lax.axis_size(axis)
    leading, last = (max(0, -steps), min(count, count - steps))
    return lax.ppermute(value, axis, [(source, source + steps) for source in range(leading, last)])


def lag_table(offsets, tap_gains, first_column, width, columns_all):
    bands = offsets.shape[0]
    lag_range = jnp.arange(MAXLAG + 1, dtype=jnp.int32)
    hits = (offsets[:, :, None] == lag_range[None, None, :]).astype(jnp.float32)
    band_table = jnp.sum(tap_gains[:, :, None] * hits, axis=1)
    column_band = (first_column + jnp.arange(width, dtype=jnp.int32)) // (columns_all // bands)
    selector = (column_band[None, :] == jnp.arange(bands, dtype=jnp.int32)[:, None]).astype(
        jnp.float32
    )
    return jnp.dot(band_table.T, selector, precision=lax.Precision.HIGHEST)


def arrange(panel, block_orders, offsets, tap_gains, first_column, columns_all):
    tr_count = lax.axis_size("tr")
    tr_rows, width = panel.shape
    pieces = panel.reshape(tr_count, tr_rows // tr_count, width)
    spread = lax.all_to_all(pieces, "tr", split_axis=0, concat_axis=0, tiled=True)
    outgoing = jnp.take(spread, block_orders, axis=0)
    arrived = lax.all_to_all(outgoing, "tr", split_axis=1, concat_axis=1, tiled=True)
    moved = arrived.reshape(block_orders.shape[0], tr_rows, width)
    series = jnp.concatenate([panel[None], moved], axis=0)
    rim = passed_along(series[:, tr_rows - MAXLAG :, :], "tr", 1)
    extended = jnp.concatenate([rim, series], axis=1)
    table = lag_table(offsets, tap_gains, first_column, width, columns_all)
    total = jnp.zeros(series.shape, jnp.float32)
    for lag in range(MAXLAG + 1):
        window = extended[:, MAXLAG - lag : MAXLAG - lag + tr_rows, :].astype(jnp.float32)
        total = total + table[lag][None, None, :] * window
    return total.astype(jnp.bfloat16)


def on_device(features, block_orders, offsets, tap_gains, weights, signal, block_owner):
    weight = weights[0]
    columns_all = weight.shape[0]
    panel = lax.all_gather(features, "subj", axis=1, tiled=True)
    filtered = arrange(panel, block_orders, offsets, tap_gains, 0, columns_all)
    predicted = jnp.einsum("ctf,fv->ctv", filtered, weight, preferred_element_type=jnp.float32)
    measured = signal[0].astype(jnp.float32)
    residual = measured[None] - predicted
    squared = residual * residual
    energy = jnp.mean(squared, axis=2).T[None]
    stats = jnp.concatenate(
        [jnp.sum(squared, axis=1), jnp.sum(measured * measured, axis=0)[None]], axis=0
    )
    conditions = stats.shape[0] - 1
    owners = block_owner[0, :, 0]
    blocks = owners.shape[0]
    order = jnp.arange(blocks, dtype=jnp.int32)
    same_owner = (owners[:, None] == owners[None, :]) & (order[:, None] > order[None, :])
    rank = jnp.sum(same_owner.astype(jnp.int32), axis=1)
    slot = owners * CAP + rank
    totals = lax.psum(stats, "tr")
    fit = jnp.log((totals[:conditions] + epsilon) / (totals[conditions] + epsilon)[None, :])
    block_fit = jnp.mean(fit.reshape(conditions, blocks, VB), axis=2)
    wanted = lax.axis_index("tr") * CAP + jnp.arange(CAP, dtype=jnp.int32)
    selector = (slot[None, :] == wanted[:, None]).astype(jnp.float32)
    scores = jnp.dot(selector, block_fit.T, precision=lax.Precision.HIGHEST)
    return (energy, scores[None])


def solution(mesh):
    placed = (
        P("tr", "subj"),
        P(),
        P(),
        P(),
        P("subj", None, None),
        P("subj", "tr", None),
        P("subj", None, None),
    )
    return jax.shard_map(
        on_device,
        mesh=mesh,
        in_specs=placed,
        out_specs=(P("subj", "tr", None), P("subj", "tr", None)),
        check_vma=False,
    )
```

profile of v0, /device:TPU:1, one launch (start us, length us, event | category | flops | bytes accessed | tf_op | source)
XLA Modules:
  0.0 355.0 jit_solution(7565294800211539348)
XLA Ops:
  0.6 26.2 %all_gather.3 = bf16[64,2048]{1,0:T(8,128)(2,1)S(1)} all-gather(bf16[64,256]{1,0:T(8,128)(2,1)} %param.7), channel_id=1, replica_groups=mesh['subj'=8,'tr'=64] {'subj'}, dimensions={1}, use_global_device_ids=true | all-gather | bytes 294912 | tf_op jit(solution)/shard_map/all_gather | solution.py:54
  26.8 0.5 broadcast.73
  27.3 0.8 reduce.1
  28.1 0.9 reshape.84
  29.0 16.8 %all-to-all-start = ((bf16[64,2,1024]{2,1,0:T(2,128)(2,1)}), bf16[64,2,1024]{2,1,0:T(2,128)(2,1)S(1)}, u32[]{:S(2)}, u32[]{:S(2)}) async-start(bf16[64,2,1024]{2,1,0:T(2,128)(2,1)} %reshape.84), calls=%async_computation | async-start | bytes 524288 | tf_op jit(solution)/shard_map/all_to_all | solution.py:36
  45.8 0.7 compare_select_fusion
  46.5 0.1 reshape.74
  46.6 0.7 compare_and_fusion
  47.2 0.1 copy.22
  47.4 11.6 %all-to-all-done = bf16[64,2,1024]{2,1,0:T(2,128)(2,1)S(1)} async-done(((bf16[64,2,1024]{2,1,0:T(2,128)(2,1)}), bf16[64,2,1024]{2,1,0:T(2,128)(2,1)S(1)}, u32[]{:S(2)}, u32[]{:S(2)}) %all-to-all-start) | async-done | bytes 262176 | tf_op jit(solution)/shard_map/all_to_all | solution.py:36
  58.9 0.2 reshape.85
  59.2 0.2 copy.35
  59.3 1.4 gather_fusion
  60.7 1.9 copy_select_fusion
  62.7 4.7 %all-to-all-start.1 = ((bf16[4,64,1,2048]{3,0,2,1:T(4,128)(2,1)}), bf16[4,64,1,2048]{3,0,2,1:T(4,128)(2,1)S(1)}, u32[]{:S(2)}, u32[]{:S(2)}) async-start(bf16[4,64,1,2048]{3,0,2,1:T(4,128)(2,1)} %copy_select_fusion), calls=%async_computation.1 | async-start | bytes 2097152 | tf_op jit(solution)/shard_map/all_to_all | solution.py:38
  67.4 0.4 copy.25
  67.9 0.1 select_reduce_fusion
  68.0 0.2 convert_reduce_fusion
  68.1 0.3 fusion.14
  68.5 26.9 %all-to-all-done.1 = bf16[4,64,1,2048]{3,0,2,1:T(4,128)(2,1)S(1)} async-done(((bf16[4,64,1,2048]{3,0,2,1:T(4,128)(2,1)}), bf16[4,64,1,2048]{3,0,2,1:T(4,128)(2,1)S(1)}, u32[]{:S(2)}, u32[]{:S(2)}) %all-to-all-start.1) | async-done | bytes 1048608 | tf_op jit(solution)/shard_map/all_to_all | solution.py:38
  95.4 0.1 fusion.9
  95.5 4.3 %collective-permute-start = (bf16[5,8,2048]{2,0,1:T(8,128)(2,1)S(1)}, bf16[5,8,2048]{2,0,1:T(8,128)(2,1)S(1)}, u32[]{:S(2)}, u32[]{:S(2)}) collective-permute-start(bf16[5,8,2048]{2,0,1:T(8,128)(2,1)S(1)} %fusion.9), channel_id=1, source_target_pairs={{0,1},{1,2},{2,3},{3,4},{4,5},{5,6},{6,7},{7,8},{8,9},{9,10},{10,1... | collective-permute-start | bytes 491528 | tf_op jit(solution)/shard_map/ppermute | solution.py:17
  99.9 3.2 collective-permute-done
  103.2 1.1 maximum_maximum_fusion
  104.3 5.1 %add_convert_fusion = bf16[5,64,2048]{2,0,1:T(8,128)(2,1)S(1)} fusion(bf16[4,64,2048]{2,0,1:T(4,128)(2,1)S(1)} %bitcast.41, bf16[1,64,2048]{2,0,1:T(2,128)(2,1)S(1)} %copy.25, bf16[5,72,2048]{2,0,1:T(8,128)(2,1)S(1)} %maximum_maximum_fusion, f32[2048]{0:T(1024)S(1)} %bitcast.46, f32[2048]{0:T(1024)S(1)} %bitcast.47, f32[2048]{0:T(1024)S(1)} %bitcast.48, ...), kind=kLoop, calls=%fused_computation.3 | loop fusion | flops 19660800 | bytes 13180928 | tf_op jit(solution)/shard_map/convert_element_type | solution.py:48
  109.4 2.3 fusion.25
  111.7 241.0 %psum.7 = f32[6,1024]{1,0:T(8,128)S(1)} all-reduce(f32[6,1024]{1,0:T(8,128)S(1)} %pad_maximum_fusion.1), channel_id=1, replica_groups=mesh['subj'=8,'tr'=64] {'tr'}, use_global_device_ids=true, to_apply=%region_5.6 | all-reduce | flops 6144 | bytes 49152 | tf_op jit(solution)/shard_map/psum | solution.py:71
  352.7 0.7 reshape.68
  353.4 0.2 reduce_sum.59
  353.6 0.2 convolution_bitcast_fusion
  353.8 0.7 copy.27
  354.5 0.6 broadcast_in_dim.39
  (21 shorter events, 0.2 us)
Async XLA Ops:
  29.0 30.0 %all-to-all-start = ((bf16[64,2,1024]{2,1,0:T(2,128)(2,1)}), bf16[64,2,1024]{2,1,0:T(2,128)(2,1)S(1)}, u32[]{:S(2)}, u32[]{:S(2)}) async-start(bf16[64,2,1024]{2,1,0:T(2,128)(2,1)} %reshape.84), calls=%async_computation | async-start | bytes 524288 | tf_op jit(solution)/shard_map/all_to_all | solution.py:36
  60.7 7.1 %copy-start.2 = (f32[4,4]{1,0:T(4,128)S(1)}, f32[4,4]{1,0:T(4,128)}, u32[]{:S(2)}) copy-start(f32[4,4]{1,0:T(4,128)} %param.10) | copy-start | bytes 196
  60.7 7.1 %copy-start.3 = (s32[4,4]{1,0:T(4,128)S(1)}, s32[4,4]{1,0:T(4,128)}, u32[]{:S(2)}) copy-start(s32[4,4]{1,0:T(4,128)} %param.9) | copy-start | bytes 196
  60.7 7.2 %copy-start.1 = (s32[1,256,1]{1,2,0:T(1,128)S(1)}, s32[1,256,1]{1,2,0:T(1,128)}, u32[]{:S(2)}) copy-start(s32[1,256,1]{1,2,0:T(1,128)} %param.13) | copy-start | bytes 3076
  60.7 7.7 %copy-start = (bf16[1,64,1024]{2,1,0:T(8,128)(2,1)S(1)}, bf16[1,64,1024]{2,1,0:T(8,128)(2,1)}, u32[]{:S(2)}) copy-start(bf16[1,64,1024]{2,1,0:T(8,128)(2,1)} %param.12) | copy-start | bytes 393220
  62.7 32.7 %all-to-all-start.1 = ((bf16[4,64,1,2048]{3,0,2,1:T(4,128)(2,1)}), bf16[4,64,1,2048]{3,0,2,1:T(4,128)(2,1)S(1)}, u32[]{:S(2)}, u32[]{:S(2)}) async-start(bf16[4,64,1,2048]{3,0,2,1:T(4,128)(2,1)} %copy_select_fusion), calls=%async_computation.1 | async-start | bytes 2097152 | tf_op jit(solution)/shard_map/all_to_all | solution.py:38
  95.5 7.7 %collective-permute-start = (bf16[5,8,2048]{2,0,1:T(8,128)(2,1)S(1)}, bf16[5,8,2048]{2,0,1:T(8,128)(2,1)S(1)}, u32[]{:S(2)}, u32[]{:S(2)}) collective-permute-start(bf16[5,8,2048]{2,0,1:T(8,128)(2,1)S(1)} %fusion.9), channel_id=1, source_target_pairs={{0,1},{1,2},{2,3},{3,4},{4,5},{5,6},{6,7},{7,8},{8,9},{9,10},{10,1... | collective-permute-start | bytes 491528 | tf_op jit(solution)/shard_map/ppermute | solution.py:17
  104.2 5.1 %copy-start.4 = (bf16[1,2048,1024]{2,1,0:T(8,128)(2,1)S(1)}, bf16[1,2048,1024]{2,1,0:T(8,128)(2,1)}, u32[]{:S(2)}) copy-start(bf16[1,2048,1024]{2,1,0:T(8,128)(2,1)} %param.11) | copy-start | bytes 12582916
where the time goes:
time: 360 us; the launch traced here: 355 us
  blocking collectives  267 us (74%)
  waiting for transfers between devices  41.7 us (12%)
  starting transfers between devices  25.9 us (7%)
  other arithmetic  11 us (3%)
  local copies, waits for them, and re-layouts  5.74 us (2%)
    psum x1, blocking collectives, on_device(): totals = lax.psum(stats, 'tr')  241 us
    all_to_all x1, waiting for transfers between devices, arrange(): lax.all_to_all(outgoing, 'tr', split_axis=1, concat_axis=1, tiled=True)  26.9 us
    all_gather x1, blocking collectives, on_device(): panel = lax.all_gather(features, 'subj', axis=1, tiled=True)  26.2 us
    all_to_all x1, starting transfers between devices, arrange(): lax.all_to_all(pieces, 'tr', split_axis=0, concat_axis=0, tiled=True)  16.8 us
    all_to_all x1, waiting for transfers between devices, arrange(): lax.all_to_all(pieces, 'tr', split_axis=0, concat_axis=0, tiled=True)  11.6 us
  transfers between devices with their start and end apart: 3, of which 3 were waited for; matrix products, arithmetic and copies ran while one was open for 1% of the time, Pallas kernels for 0%

commit v1 on v0

v1 whole, which is shorter than its diff:
```python
import jax
import jax.numpy as jnp
from jax import lax
from jax.experimental import pallas as pl
from jax.experimental.pallas import tpu as pltpu
from jax.sharding import PartitionSpec as P

MAXLAG = 8
NLAG = 4
VB = 4
CAP = 8
NT = 64
NZ = 8
NY = 8
NX = 8
KC = 5
ROWS = 64
FZ = 256
F = 2048
V = 1024
BAND_DEVICES = 2
LANES = 128
VT = V // LANES
EPS = 1e-06

MESH = pl.DeviceIdType.MESH
F32 = jnp.float32
BF16 = jnp.bfloat16


def dot(a, b):
    return jnp.dot(a, b, preferred_element_type=F32)


def iota(shape, axis):
    return lax.broadcasted_iota(jnp.int32, shape, axis)


def wait_for(ref, sem):
    pltpu.make_async_copy(ref, ref, sem).wait()


def kernel(
    feat_hbm, orders, offs, gains, w_hbm, sig_hbm, owner,
    energy, scores,
    feat, sig, w, pad, send_f, recv_f, zbuf, rim, wide, send_s, recv_s, sall, pred,
    send_r, recv_r, c1_send, c1_recv, c2, c3, sel,
    local_sem, rim_ss, rim_rs, f_ss, f_rs, s_ss, s_rs, z_ss, z_rs, r_ss, r_rs,
    c1_ss, c1_rs, c2_ss, c2_rs, c3_ss, c3_rs,
):
    z = lax.axis_index("subj")
    me = lax.axis_index("tr")
    y = me // NX
    xc = me % NX

    def send(src, dst, ss, rs, **where):
        pltpu.make_async_remote_copy(
            src_ref=src, dst_ref=dst, send_sem=ss, recv_sem=rs,
            device_id=where, device_id_type=MESH,
        ).start()

    feat_copy = pltpu.make_async_copy(feat_hbm, feat, local_sem.at[0])
    sig_copy = pltpu.make_async_copy(sig_hbm.at[0], sig, local_sem.at[1])
    w_copy = pltpu.make_async_copy(w_hbm.at[0], w, local_sem.at[2])
    feat_copy.start()
    sig_copy.start()
    w_copy.start()

    barrier = pltpu.get_barrier_semaphore()

    def greet_tr(i, carry):
        pl.semaphore_signal(barrier, inc=1, device_id={"tr": (me + i) % NT}, device_id_type=MESH)
        return carry

    def greet_subj(i, carry):
        pl.semaphore_signal(barrier, inc=1, device_id={"subj": (z + i) % NZ}, device_id_type=MESH)
        return carry

    lax.fori_loop(1, NZ, greet_subj, 0)
    lax.fori_loop(1, NT, greet_tr, 0)

    feat_copy.wait()
    pad[0:MAXLAG] = jnp.zeros((MAXLAG, FZ), F32)
    pad[MAXLAG + ROWS:] = jnp.zeros((MAXLAG, FZ), F32)
    pad[MAXLAG:MAXLAG + ROWS] = feat[...].astype(F32)
    band = z // BAND_DEVICES
    total = jnp.zeros((ROWS + MAXLAG, FZ), F32)
    for lag in range(MAXLAG + 1):
        gain = jnp.float32(0.0)
        for tap in range(NLAG):
            gain = gain + jnp.where(offs[band, tap] == lag, gains[band, tap], jnp.float32(0.0))
        total = total + gain * pad[MAXLAG - lag:MAXLAG - lag + ROWS + MAXLAG]
    for j in range(FZ // LANES):
        send_f[:, j, :] = total[:ROWS, j * LANES:(j + 1) * LANES]
    rim[z] = total[ROWS:].astype(BF16)

    pl.semaphore_wait(barrier, NT - 1 + NZ - 1)

    def send_rim(i, carry):
        send(rim.at[z], rim.at[z], rim_ss, rim_rs, subj=(z + i) % NZ)
        return carry

    def send_feature(i, carry):
        to = (me + i) % NT
        send(send_f.at[to], recv_f.at[me], f_ss, f_rs, tr=to)
        return carry

    lax.fori_loop(1, NT, send_feature, 0)
    lax.fori_loop(1, NZ, send_rim, 0)
    recv_f[me] = send_f[me]

    sig_copy.wait()
    for j in range(VT):
        wide[:, j, :] = sig[:, j * LANES:(j + 1) * LANES].astype(F32)
    send_s[...] = wide[...].astype(BF16)

    def send_signal(i, carry):
        to = (me + i) % NT
        send(send_s.at[to], recv_s.at[me], s_ss, s_rs, tr=to)
        return carry

    lax.fori_loop(1, NT, send_signal, 0)
    recv_s[me] = send_s[me]

    wait_for(recv_f.at[pl.ds(0, NT - 1)], f_rs)
    for j in range(FZ // LANES):
        zbuf[z, :, j * LANES:(j + 1) * LANES] = recv_f[:, j, :].astype(BF16)

    def send_columns(i, carry):
        to = (z + i) % NZ
        send(zbuf.at[z], zbuf.at[z], z_ss, z_rs.at[z], subj=to)
        return carry

    lax.fori_loop(1, NZ, send_columns, 0)

    wait_for(rim.at[pl.ds(0, NZ - 1)], rim_rs)
    w_copy.wait()
    part = dot(rim[0], w[0:FZ])
    for k in range(1, NZ):
        part = part + dot(rim[k], w[k * FZ:(k + 1) * FZ])
    for j in range(VT):
        send_r[:, j, :] = part[:, j * LANES:(j + 1) * LANES]

    def send_part(i, carry):
        @pl.when(i != me)
        def _():
            send(send_r.at[i], recv_r.at[me], r_ss, r_rs, tr=i)
        return carry

    lax.fori_loop(0, MAXLAG, send_part, 0)

    @pl.when(me < MAXLAG)
    def _():
        recv_r[me] = send_r[me]

    blocks = owner.shape[1]
    owned = jnp.broadcast_to(owner[...] == me, (CAP, blocks))
    before = (iota((blocks, blocks), 0) < iota((blocks, blocks), 1)).astype(F32).astype(BF16)
    rank = dot(owned.astype(F32).astype(BF16), before)
    chosen = jnp.where(owned & (rank == iota((CAP, blocks), 0).astype(F32)), 1.0, 0.0).astype(BF16)
    spread = (iota((blocks, V), 1) // VB == iota((blocks, V), 0)).astype(F32).astype(BF16)
    sel[...] = dot(chosen, spread)

    def place(c):
        if c == 0:
            return iota((NT, NT), 0) == iota((NT, NT), 1)
        return jnp.broadcast_to(orders[c - 1:c, :], (NT, NT)) == iota((NT, NT), 0)

    wait_for(recv_s.at[pl.ds(0, NT - 1)], s_rs)
    wide[...] = recv_s[...].astype(F32)
    tss = []
    for j in range(VT):
        column = wide[:, j, :]
        sall[0, :, j * LANES:(j + 1) * LANES] = column
        tss.append(jnp.sum(column * column, axis=0, keepdims=True))
    rows = sall[0].astype(BF16)
    for c in range(1, KC):
        sall[c] = dot(place(c).astype(F32).astype(BF16), rows)

    @pl.when(me < MAXLAG)
    def _():
        wait_for(recv_r.at[pl.ds(0, NT - 1)], r_rs)
        after = (iota((NT, NT), 0) == iota((NT, NT), 1) + 1).astype(F32).astype(BF16)
        for j in range(VT):
            pred[:, j * LANES:(j + 1) * LANES] = recv_r[:, j, :]
        high = pred[...].astype(BF16)
        low = (pred[...] - high.astype(F32)).astype(BF16)
        for c in range(KC):
            placed = place(c).astype(F32).astype(BF16)
            shifted = dot(placed, after).astype(BF16)
            behind = lax.dot_general(
                shifted, placed, (((1,), (1,)), ((), ())), preferred_element_type=F32
            ).astype(BF16)
            sall[c] = sall[c] - (dot(behind, high) + dot(behind, low))

    def weight(k):
        return w[pl.ds(pl.multiple_of(k * FZ, FZ), FZ), :]

    pred[...] = dot(zbuf[z], weight(z))
    for i in (1, 7, 2, 6, 3, 5, 4):
        k = (z + i) % NZ
        wait_for(zbuf.at[k], z_rs.at[k])
        pred[...] += dot(zbuf[k], weight(k))

    over = [jnp.zeros((NT, LANES), F32) for _ in range(KC)]
    for j in range(VT):
        value = pred[:, j * LANES:(j + 1) * LANES]
        stats = []
        for c in range(KC):
            residual = sall[c, :, j * LANES:(j + 1) * LANES] - value
            squared = residual * residual
            over[c] = over[c] + squared
            stats.append(jnp.sum(squared, axis=0, keepdims=True))
        stats = stats + [tss[j], jnp.zeros((2, LANES), F32)]
        c1_send[j, 0:8, :] = jnp.concatenate(stats, axis=0)
    placed_energy = []
    for c in range(KC):
        column = jnp.sum(over[c], axis=1, keepdims=True)
        placed_energy.append(
            jnp.sum(jnp.where(place(c), jnp.broadcast_to(column, (NT, NT)), 0.0), axis=0, keepdims=True)
        )
    placed_energy = jnp.concatenate(placed_energy + [jnp.zeros((3, NT), F32)], axis=0)
    placed_energy = jnp.concatenate([placed_energy, jnp.zeros((8, LANES - NT), F32)], axis=1)
    for j in range(NY):
        c1_send[j, 8:16, :] = placed_energy

    def send_c1(i, carry):
        to = (y + i) % NY
        send(c1_send.at[to], c1_recv.at[y], c1_ss, c1_rs, tr=to * NX + xc)
        return carry

    lax.fori_loop(1, NY, send_c1, 0)
    c1_recv[y] = c1_send[y]
    wait_for(c1_recv.at[pl.ds(0, NY - 1)], c1_rs)
    lane = iota((8, LANES), 1)
    tile = c1_recv[0, 0:8, :]
    for k in range(1, NY):
        tile = tile + c1_recv[k, 0:8, :]
    packed = jnp.zeros((8, LANES), F32)
    for k in range(NY):
        moved = pltpu.roll(c1_recv[k, 8:16, :], ((k - y) * NX + LANES) % LANES, 1)
        packed = jnp.where(lane // NX == k, moved, packed)
    c2[xc, 0:8, :] = tile
    c2[xc, 8:16, :] = packed

    def send_c2(i, carry):
        send(c2.at[xc], c2.at[xc], c2_ss, c2_rs, tr=y * NX + (xc + i) % NX)
        return carry

    lax.fori_loop(1, NX, send_c2, 0)
    wait_for(c2.at[pl.ds(0, NX - 1)], c2_rs)
    tile = c2[0, 0:8, :]
    for k in range(1, NX):
        tile = tile + c2[k, 0:8, :]
    fit = jnp.log((tile + EPS) / (tile[KC:KC + 1] + EPS))
    c3[y] = fit

    def send_c3(i, carry):
        send(c3.at[y], c3.at[y], c3_ss, c3_rs, tr=((y + i) % NY) * NX + xc)
        return carry

    lax.fori_loop(1, NY, send_c3, 0)

    mean = jnp.zeros((8, LANES), F32)
    for k in range(NX):
        moved = pltpu.roll(c2[k, 8:16, :], (k - xc + LANES) % LANES, 1)
        mean = jnp.where(lane % NX == k, moved, mean)
    mean = mean * (1.0 / V)
    for c in range(KC):
        energy[c, :, :] = mean[c:c + 1, :NT]

    wait_for(c3.at[pl.ds(0, NY - 1)], c3_rs)
    result = jnp.zeros((8, LANES), F32)
    for k in range(CAP):
        picked = jnp.zeros((8, LANES), F32)
        for j in range(NY):
            picked = picked + c3[j] * sel[k:k + 1, j * LANES:(j + 1) * LANES]
        column = jnp.sum(picked, axis=1, keepdims=True)
        result = jnp.where(lane == k, jnp.broadcast_to(column, (8, LANES)), result)
    result = result * (1.0 / VB)
    for c in range(KC):
        scores[c, :, :] = result[c:c + 1, :CAP]

    wait_for(rim.at[pl.ds(0, NZ - 1)], rim_ss)
    wait_for(send_f.at[pl.ds(0, NT - 1)], f_ss)
    wait_for(send_s.at[pl.ds(0, NT - 1)], s_ss)
    wait_for(zbuf.at[pl.ds(0, NZ - 1)], z_ss)
    wait_for(c1_send.at[pl.ds(0, NY - 1)], c1_ss)
    wait_for(c2.at[pl.ds(0, NX - 1)], c2_ss)
    wait_for(c3.at[pl.ds(0, NY - 1)], c3_ss)

    @pl.when(me < MAXLAG)
    def _():
        wait_for(send_r.at[pl.ds(0, MAXLAG - 1)], r_ss)

    @pl.when(me >= MAXLAG)
    def _():
        wait_for(send_r, r_ss)


def on_device(features, block_orders, offsets, tap_gains, weights, signal, block_owner):
    anywhere = pl.BlockSpec(memory_space=pl.ANY)
    vmem = pl.BlockSpec(memory_space=pltpu.VMEM)
    smem = pl.BlockSpec(memory_space=pltpu.SMEM)
    sem = pltpu.SemaphoreType.DMA
    owner = block_owner.reshape(1, block_owner.shape[1])
    energy, scores = pl.pallas_call(
        kernel,
        out_shape=(
            jax.ShapeDtypeStruct((KC, 1, NT), F32),
            jax.ShapeDtypeStruct((KC, 1, CAP), F32),
        ),
        in_specs=[anywhere, vmem, smem, smem, anywhere, anywhere, vmem],
        out_specs=(vmem, vmem),
        scratch_shapes=[
            pltpu.VMEM((ROWS, FZ), BF16),
            pltpu.VMEM((ROWS, V), BF16),
            pltpu.VMEM((F, V), BF16),
            pltpu.VMEM((ROWS + 2 * MAXLAG, FZ), F32),
            pltpu.VMEM((NT, FZ // LANES, LANES), F32),
            pltpu.VMEM((NT, FZ // LANES, LANES), F32),
            pltpu.VMEM((NZ, NT, FZ), BF16),
            pltpu.VMEM((NZ, MAXLAG, FZ), BF16),
            pltpu.VMEM((NT, VT, LANES), F32),
            pltpu.VMEM((NT, VT, LANES), BF16),
            pltpu.VMEM((NT, VT, LANES), BF16),
            pltpu.VMEM((KC, NT, V), F32),
            pltpu.VMEM((NT, V), F32),
            pltpu.VMEM((MAXLAG, VT, LANES), F32),
            pltpu.VMEM((NT, VT, LANES), F32),
            pltpu.VMEM((NY, 16, LANES), F32),
            pltpu.VMEM((NY, 16, LANES), F32),
            pltpu.VMEM((NX, 16, LANES), F32),
            pltpu.VMEM((NY, 8, LANES), F32),
            pltpu.VMEM((CAP, V), F32),
            sem((3,)),
            sem, sem, sem, sem, sem, sem, sem, sem((NZ,)), sem, sem,
            sem, sem, sem, sem, sem, sem,
        ],
        compiler_params=pltpu.CompilerParams(
            collective_id=0, has_side_effects=True, vmem_limit_bytes=40 * 1024 * 1024
        ),
    )(features, block_orders, offsets, tap_gains, weights, signal, owner)
    return jnp.transpose(energy, (1, 2, 0)), jnp.transpose(scores, (1, 2, 0))


def solution(mesh):
    placed = (
        P("tr", "subj"),
        P(),
        P(),
        P(),
        P("subj", None, None),
        P("subj", "tr", None),
        P("subj", None, None),
    )
    return jax.shard_map(
        on_device,
        mesh=mesh,
        in_specs=placed,
        out_specs=(P("subj", "tr", None), P("subj", "tr", None)),
        check_vma=False,
    )
```

time: 360 us -> 54.9 us (0.15); the launches traced: 355 us -> 54.6 us
  blocking collectives: 267 us -> 0 us
  Pallas kernels: 0 us -> 46.2 us
  waiting for transfers between devices: 41.7 us -> 0 us
  starting transfers between devices: 25.9 us -> 0 us
  other arithmetic: 11 us -> 0 us
    psum x1 -> x0, blocking collectives: 241 us -> none  [on_device(): totals = lax.psum(stats, 'tr')]
    pallas_call x0 -> x1, Pallas kernels: none -> 46.2 us  [on_device(): pl.pallas_call(kernel, out_shape=(jax.ShapeDtypeStruct((KC, 1, NT), F32),...]
    all_to_all x2 -> x0, waiting for transfers between devices: 38.5 us -> none  [the longest x1 26.9 us: arrange(): lax.all_to_all(outgoing, 'tr', split_axis=1, concat_axis=1, tiled=True)]
    all_gather x1 -> x0, blocking collectives: 26.2 us -> none  [on_device(): panel = lax.all_gather(features, 'subj', axis=1, tiled=True)]
    all_to_all x2 -> x0, starting transfers between devices: 21.5 us -> none  [the longest x1 16.8 us: arrange(): lax.all_to_all(pieces, 'tr', split_axis=0, concat_axis=0, tiled=True)]
    unnamed x14 -> x16, local copies, waits for them, and re-layouts: 1.95 us -> 7.72 us
    convert_element_type x1 -> x0, other arithmetic: 5.11 us -> none  [arrange(): return total.astype(jnp.bfloat16)]
    ppermute x1 -> x0, starting transfers between devices: 4.35 us -> none  [passed_along(): lax.ppermute(value, axis, [(source, source + steps) for source in range(l...]
  transfers between devices with their start and end apart: 3 -> 0, of which waited for: 3 -> 0; matrix products, arithmetic and copies ran while one was open for 1% -> 0% of each run, Pallas kernels for 0% -> 0%
where the time goes in v1:
time: 54.9 us; the launch traced here: 54.6 us
  Pallas kernels  46.2 us (84%)
  local copies, waits for them, and re-layouts  7.72 us (14%)
  between operations  0.66 us (1%)
    pallas_call x1, Pallas kernels, on_device(): pl.pallas_call(kernel, out_shape=(jax.ShapeDtypeStruct((KC, 1, NT), F32),...  46.2 us
    unnamed x16, local copies, waits for them, and re-layouts  7.72 us

profile of v1, /device:TPU:1, one launch (start us, length us, event | category | flops | bytes accessed | tf_op | source)
XLA Modules:
  0.0 54.6 jit_solution(8591143359396472149)
XLA Ops:
  0.6 0.0 copy-start
  0.6 2.2 %copy-done = bf16[1,2048,1024]{2,1,0:T(8,128)(2,1)S(1)} copy-done((bf16[1,2048,1024]{2,1,0:T(8,128)(2,1)S(1)}, bf16[1,2048,1024]{2,1,0:T(8,128)(2,1)}, u32[]{:S(2)}) %copy-start) | copy-done | bytes 4194328
  2.8 0.0 copy-start.1
  2.8 0.9 %copy-done.1 = bf16[1,64,1024]{2,1,0:T(8,128)(2,1)S(1)} copy-done((bf16[1,64,1024]{2,1,0:T(8,128)(2,1)S(1)}, bf16[1,64,1024]{2,1,0:T(8,128)(2,1)}, u32[]{:S(2)}) %copy-start.1) | copy-done | bytes 131096
  3.7 0.0 copy-start.2
  3.7 0.8 %copy-done.2 = bf16[64,256]{1,0:T(8,128)(2,1)S(1)} copy-done((bf16[64,256]{1,0:T(8,128)(2,1)S(1)}, bf16[64,256]{1,0:T(8,128)(2,1)}, u32[]{:S(2)}) %copy-start.2) | copy-done | bytes 32792
  4.5 0.0 copy-start.3
  4.5 0.7 %copy-done.3 = s32[4,64]{1,0:T(4,128)S(1)} copy-done((s32[4,64]{1,0:T(4,128)S(1)}, s32[4,64]{1,0:T(4,128)}, u32[]{:S(2)}) %copy-start.3) | copy-done | bytes 1048
  5.2 0.0 copy-start.4
  5.2 0.7 %copy-done.4 = s32[4,4]{1,0:T(4,128)S(1)} copy-done((s32[4,4]{1,0:T(4,128)S(1)}, s32[4,4]{1,0:T(4,128)}, u32[]{:S(2)}) %copy-start.4) | copy-done | bytes 88
  5.8 0.0 copy-start.5
  5.9 0.7 %copy-done.5 = f32[4,4]{1,0:T(4,128)S(1)} copy-done((f32[4,4]{1,0:T(4,128)S(1)}, f32[4,4]{1,0:T(4,128)}, u32[]{:S(2)}) %copy-start.5) | copy-done | bytes 88
  6.5 0.0 copy-start.6
  6.5 0.7 %copy-done.6 = s32[1,256,1]{1,2,0:T(1,128)S(1)} copy-done((s32[1,256,1]{1,2,0:T(1,128)S(1)}, s32[1,256,1]{1,2,0:T(1,128)}, u32[]{:S(2)}) %copy-start.6) | copy-done | bytes 1048
  7.2 46.2 %shard_map.86 = (f32[5,1,64]{2,1,0:T(1,128)S(1)}, f32[5,1,8]{2,1,0:T(1,128)S(1)}) custom-call(bf16[64,256]{1,0:T(8,128)(2,1)S(1)} %copy-done.2, s32[4,64]{1,0:T(4,128)S(1)} %copy-done.3, s32[4,4]{1,0:T(4,128)S(1)} %copy-done.4, f32[4,4]{1,0:T(4,128)S(1)} %copy-done.5, bf16[1,2048,1024]{2,1,0:T(8,128)(2,1)S(1)} %copy-done, ...), custom_call_target="tpu_custom_call" | custom-call | tf_op jit(solution)/shard_map/pallas_call | solution.py:307
  53.4 0.6 %copy.11 = f32[1,64,5]{1,0,2:T(1,128)} copy(f32[1,64,5]{1,0,2:T(1,128)S(1)} %bitcast.4) | data formatting | bytes 2560
  54.0 0.6 %copy.12 = f32[1,8,5]{1,0,2:T(1,128)} copy(f32[1,8,5]{1,0,2:T(1,128)S(1)} %bitcast.3) | data formatting | bytes 320
Async XLA Ops:
  0.6 2.2 %copy-start = (bf16[1,2048,1024]{2,1,0:T(8,128)(2,1)S(1)}, bf16[1,2048,1024]{2,1,0:T(8,128)(2,1)}, u32[]{:S(2)}) copy-start(bf16[1,2048,1024]{2,1,0:T(8,128)(2,1)} %w_hbm.1) | copy-start | bytes 12582916
  2.8 0.9 %copy-start.1 = (bf16[1,64,1024]{2,1,0:T(8,128)(2,1)S(1)}, bf16[1,64,1024]{2,1,0:T(8,128)(2,1)}, u32[]{:S(2)}) copy-start(bf16[1,64,1024]{2,1,0:T(8,128)(2,1)} %sig_hbm.1) | copy-start | bytes 393220
  3.7 0.8 %copy-start.2 = (bf16[64,256]{1,0:T(8,128)(2,1)S(1)}, bf16[64,256]{1,0:T(8,128)(2,1)}, u32[]{:S(2)}) copy-start(bf16[64,256]{1,0:T(8,128)(2,1)} %feat_hbm.1) | copy-start | bytes 98308
  4.5 0.7 %copy-start.3 = (s32[4,64]{1,0:T(4,128)S(1)}, s32[4,64]{1,0:T(4,128)}, u32[]{:S(2)}) copy-start(s32[4,64]{1,0:T(4,128)} %orders.1) | copy-start | bytes 3076
  5.2 0.7 %copy-start.4 = (s32[4,4]{1,0:T(4,128)S(1)}, s32[4,4]{1,0:T(4,128)}, u32[]{:S(2)}) copy-start(s32[4,4]{1,0:T(4,128)} %offs.1) | copy-start | bytes 196
  5.8 0.7 %copy-start.5 = (f32[4,4]{1,0:T(4,128)S(1)}, f32[4,4]{1,0:T(4,128)}, u32[]{:S(2)}) copy-start(f32[4,4]{1,0:T(4,128)} %gains.1) | copy-start | bytes 196
  6.5 0.7 %copy-start.6 = (s32[1,256,1]{1,2,0:T(1,128)S(1)}, s32[1,256,1]{1,2,0:T(1,128)}, u32[]{:S(2)}) copy-start(s32[1,256,1]{1,2,0:T(1,128)} %param.13) | copy-start | bytes 3076

commit v2 on v1

v2 whole, which is shorter than its diff:
```python
import jax
import jax.numpy as jnp
from jax import lax
from jax.experimental import pallas as pl
from jax.experimental.pallas import tpu as pltpu
from jax.sharding import PartitionSpec as P

MAXLAG = 8
NLAG = 4
VB = 4
CAP = 8
NT = 64
NZ = 8
NY = 8
NX = 8
KC = 5
ROWS = 64
FZ = 256
F = 2048
V = 1024
BAND_DEVICES = 2
LANES = 128
VT = V // LANES
EPS = 1e-06

MESH = pl.DeviceIdType.MESH
F32 = jnp.float32
BF16 = jnp.bfloat16


def dot(a, b):
    return jnp.dot(a, b, preferred_element_type=F32)


def iota(shape, axis):
    return lax.broadcasted_iota(jnp.int32, shape, axis)


def wait_for(ref, sem):
    pltpu.make_async_copy(ref, ref, sem).wait()


def kernel(
    feat_hbm, orders_hbm, offs_hbm, gains_hbm, w_hbm, sig_hbm, owner_hbm,
    energy, scores,
    orders, offs, gains, owner, feat, sig, w, pad, send_f, recv_f, zbuf, rim, wide, send_s, recv_s, sall, pred,
    send_r, recv_r, by_owner, kept, lhs, send_m, recv_m,
    local_sem, rim_ss, rim_rs, f_ss, f_rs, s_ss, s_rs, z_ss, z_rs, r_ss, r_rs,
    m_ss, m_rs,
):
    z = lax.axis_index("subj")
    me = lax.axis_index("tr")
    y = me // NX
    xc = me % NX

    def send(src, dst, ss, rs, **where):
        pltpu.make_async_remote_copy(
            src_ref=src, dst_ref=dst, send_sem=ss, recv_sem=rs,
            device_id=where, device_id_type=MESH,
        ).start()

    leaving = []

    feat_copy = pltpu.make_async_copy(feat_hbm, feat, local_sem.at[0])
    offs_copy = pltpu.make_async_copy(offs_hbm, offs, local_sem.at[3])
    gains_copy = pltpu.make_async_copy(gains_hbm, gains, local_sem.at[4])
    sig_copy = pltpu.make_async_copy(sig_hbm.at[0], sig, local_sem.at[1])
    orders_copy = pltpu.make_async_copy(orders_hbm, orders, local_sem.at[5])
    owner_copy = pltpu.make_async_copy(owner_hbm, owner, local_sem.at[6])
    w_copy = pltpu.make_async_copy(w_hbm.at[0], w, local_sem.at[2])
    for copy in (feat_copy, offs_copy, gains_copy, sig_copy, orders_copy, owner_copy, w_copy):
        copy.start()

    barrier = pltpu.get_barrier_semaphore()

    def greet_tr(i, carry):
        pl.semaphore_signal(barrier, inc=1, device_id={"tr": (me + i) % NT}, device_id_type=MESH)
        return carry

    def greet_subj(i, carry):
        pl.semaphore_signal(barrier, inc=1, device_id={"subj": (z + i) % NZ}, device_id_type=MESH)
        return carry

    lax.fori_loop(1, NZ, greet_subj, 0)
    lax.fori_loop(1, NT, greet_tr, 0)

    feat_copy.wait()
    offs_copy.wait()
    gains_copy.wait()
    pad[0:MAXLAG] = jnp.zeros((MAXLAG, FZ), F32)
    pad[MAXLAG + ROWS:] = jnp.zeros((MAXLAG, FZ), F32)
    pad[MAXLAG:MAXLAG + ROWS] = feat[...].astype(F32)
    band = z // BAND_DEVICES
    total = jnp.zeros((ROWS + MAXLAG, FZ), F32)
    for lag in range(MAXLAG + 1):
        gain = jnp.float32(0.0)
        for tap in range(NLAG):
            gain = gain + jnp.where(offs[band, tap] == lag, gains[band, tap], jnp.float32(0.0))
        total = total + gain * pad[MAXLAG - lag:MAXLAG - lag + ROWS + MAXLAG]
    for j in range(FZ // LANES):
        send_f[:, j, :] = total[:ROWS, j * LANES:(j + 1) * LANES]
    rim[z] = total[ROWS:].astype(BF16)

    pl.semaphore_wait(barrier, NT - 1 + NZ - 1)

    def send_rim(i, carry):
        send(rim.at[z], rim.at[z], rim_ss, rim_rs, subj=(z + i) % NZ)
        return carry

    def send_feature(i, carry):
        to = (me + i) % NT
        send(send_f.at[to], recv_f.at[me], f_ss, f_rs, tr=to)
        return carry

    lax.fori_loop(1, NT, send_feature, 0)
    leaving.append((send_f.at[pl.ds(0, NT - 1)], f_ss))
    lax.fori_loop(1, NZ, send_rim, 0)
    leaving.append((rim.at[pl.ds(0, NZ - 1)], rim_ss))
    recv_f[me] = send_f[me]

    sig_copy.wait()
    for j in range(VT):
        wide[:, j, :] = sig[:, j * LANES:(j + 1) * LANES].astype(F32)
    send_s[...] = wide[...].astype(BF16)

    def send_signal(i, carry):
        to = (me + i) % NT
        send(send_s.at[to], recv_s.at[me], s_ss, s_rs, tr=to)
        return carry

    lax.fori_loop(1, NT, send_signal, 0)
    leaving.append((send_s.at[pl.ds(0, NT - 1)], s_ss))
    recv_s[me] = send_s[me]

    orders_copy.wait()
    owner_copy.wait()
    blocks = owner.shape[1]
    wide_lanes = 2 * LANES
    named = (jnp.broadcast_to(owner[...], (NT, blocks)) == iota((NT, blocks), 0)).astype(F32).astype(BF16)
    spread = ((iota((blocks, V), 1) >> 2) == iota((blocks, V), 0)).astype(F32).astype(BF16)
    by_owner[...] = dot(named, spread).astype(BF16)
    same = lax.dot_general(named, named, (((0,), (0,)), ((), ())), preferred_element_type=F32)
    rank = jnp.sum(
        jnp.where(iota((blocks, blocks), 1) < iota((blocks, blocks), 0), same, 0.0), axis=1, keepdims=True
    )
    slot = ((iota((blocks, wide_lanes), 1) & 31) >> 2).astype(F32)
    ranked = (jnp.broadcast_to(rank, (blocks, wide_lanes)) == slot).astype(F32).astype(BF16)
    gathered = ((iota((V, blocks), 0) >> 2) == iota((V, blocks), 1)).astype(F32).astype(BF16)
    places = dot(gathered, ranked)
    lane = iota((V, wide_lanes), 1)
    places = jnp.where((iota((V, wide_lanes), 0) & 3) == (lane & 3), places, 0.0)
    for c in range(KC + 1):
        kept[c * V:(c + 1) * V] = jnp.where((lane >> 5) == c, places, 0.0).astype(BF16)
    mine = jnp.sum(jnp.where(owner[...] == me, 1.0, 0.0), axis=1, keepdims=True)

    wait_for(recv_f.at[pl.ds(0, NT - 1)], f_rs)
    for j in range(FZ // LANES):
        zbuf[z, :, j * LANES:(j + 1) * LANES] = recv_f[:, j, :].astype(BF16)

    def send_columns(i, carry):
        to = (z + i) % NZ
        send(zbuf.at[z], zbuf.at[z], z_ss, z_rs.at[z], subj=to)
        return carry

    lax.fori_loop(1, NZ, send_columns, 0)
    leaving.append((zbuf.at[pl.ds(0, NZ - 1)], z_ss))

    wait_for(rim.at[pl.ds(0, NZ - 1)], rim_rs)
    w_copy.wait()
    part = dot(rim[0], w[0:FZ])
    for k in range(1, NZ):
        part = part + dot(rim[k], w[k * FZ:(k + 1) * FZ])
    for j in range(VT):
        send_r[:, j, :] = part[:, j * LANES:(j + 1) * LANES]

    def send_part(i, carry):
        @pl.when(i != me)
        def _():
            send(send_r.at[i], recv_r.at[me], r_ss, r_rs, tr=i)
        return carry

    lax.fori_loop(0, MAXLAG, send_part, 0)

    @pl.when(me < MAXLAG)
    def _():
        recv_r[me] = send_r[me]

    def place(c):
        if c == 0:
            return iota((NT, NT), 0) == iota((NT, NT), 1)
        return jnp.broadcast_to(orders[c - 1:c, :], (NT, NT)) == iota((NT, NT), 0)

    def keep(c, j, value):
        columns = pl.ds(c * V + j * LANES, LANES)
        holds = by_owner[:, j * LANES:(j + 1) * LANES].astype(F32)
        for part in range(3):
            high = value.astype(BF16).astype(F32)
            lhs[part * NT:(part + 1) * NT, columns] = (holds * high).astype(BF16)
            value = value - high

    wait_for(recv_s.at[pl.ds(0, NT - 1)], s_rs)
    wide[...] = recv_s[...].astype(F32)
    for j in range(VT):
        column = wide[:, j, :]
        sall[0, :, j * LANES:(j + 1) * LANES] = column
        keep(KC, j, jnp.sum(column * column, axis=0, keepdims=True))
    rows = sall[0].astype(BF16)
    for c in range(1, KC):
        sall[c] = dot(place(c).astype(F32).astype(BF16), rows)

    @pl.when(me < MAXLAG)
    def _():
        wait_for(recv_r.at[pl.ds(0, NT - 1)], r_rs)
        after = (iota((NT, NT), 0) == iota((NT, NT), 1) + 1).astype(F32).astype(BF16)
        for j in range(VT):
            pred[:, j * LANES:(j + 1) * LANES] = recv_r[:, j, :]
        high = pred[...].astype(BF16)
        low = (pred[...] - high.astype(F32)).astype(BF16)
        for c in range(KC):
            placed = place(c).astype(F32).astype(BF16)
            shifted = dot(placed, after).astype(BF16)
            behind = lax.dot_general(
                shifted, placed, (((1,), (1,)), ((), ())), preferred_element_type=F32
            ).astype(BF16)
            sall[c] = sall[c] - (dot(behind, high) + dot(behind, low))

    def weight(k):
        return w[pl.ds(pl.multiple_of(k * FZ, FZ), FZ), :]

    pred[...] = dot(zbuf[z], weight(z))
    for i in (1, 7, 2, 6, 3, 5, 4):
        k = (z + i) % NZ
        wait_for(zbuf.at[k], z_rs.at[k])
        pred[...] += dot(zbuf[k], weight(k))

    over = [jnp.zeros((NT, LANES), F32) for _ in range(KC)]
    for j in range(VT):
        value = pred[:, j * LANES:(j + 1) * LANES]
        for c in range(KC):
            residual = sall[c, :, j * LANES:(j + 1) * LANES] - value
            squared = residual * residual
            over[c] = over[c] + squared
            keep(c, j, jnp.sum(squared, axis=0, keepdims=True))
    parts = dot(lhs[...], kept[...])
    message = parts[:NT] + parts[NT:2 * NT] + parts[2 * NT:]
    low, high = message[:, :LANES], message[:, LANES:]
    diagonal = iota((NT, NT), 0) == iota((NT, NT), 1)
    for c in range(KC):
        column = jnp.broadcast_to(jnp.sum(over[c], axis=1, keepdims=True), (NT, NT))
        row = jnp.sum(jnp.where(place(c), column, 0.0), axis=0, keepdims=True)
        column = jnp.sum(jnp.where(diagonal, jnp.broadcast_to(row, (NT, NT)), 0.0), axis=1, keepdims=True)
        high = jnp.where(iota((NT, LANES), 1) == 64 + c, jnp.broadcast_to(column, (NT, LANES)), high)
    send_m[:, 0, :] = low
    send_m[:, 1, :] = high

    def send_message(i, carry):
        to = (me + i) % NT
        send(send_m.at[to], recv_m.at[me], m_ss, m_rs, tr=to)
        return carry

    lax.fori_loop(1, NT, send_message, 0)
    leaving.append((send_m.at[pl.ds(0, NT - 1)], m_ss))
    recv_m[me] = send_m[me]
    wait_for(recv_m.at[pl.ds(0, NT - 1)], m_rs)

    high = recv_m[:, 1, :]
    turned = jnp.transpose(high) * (1.0 / V)
    for c in range(KC):
        energy[c, :, :] = turned[64 + c:65 + c, :]
    sums = [jnp.sum(recv_m[:, 0, :], axis=0, keepdims=True), jnp.sum(high, axis=0, keepdims=True)]
    sums = [sums[c // 4][:, (c % 4) * 32:(c % 4) * 32 + 32] for c in range(KC + 1)]
    fit = jnp.log((jnp.concatenate(sums[:KC], axis=0) + EPS) / (sums[KC] + EPS))
    small = iota((KC, 32), 1)
    result = jnp.zeros((KC, 32), F32)
    for k in range(CAP):
        column = jnp.sum(jnp.where((small >> 2) == k, fit, 0.0), axis=1, keepdims=True)
        result = jnp.where(small == k, jnp.broadcast_to(column, (KC, 32)), result)
    result = jnp.where(small.astype(F32) < jnp.broadcast_to(mine, (KC, 32)), result * (1.0 / VB), 0.0)
    for c in range(KC):
        scores[c, :, :] = result[c:c + 1, :CAP]

    for ref, sem in leaving:
        wait_for(ref, sem)

    @pl.when(me < MAXLAG)
    def _():
        wait_for(send_r.at[pl.ds(0, MAXLAG - 1)], r_ss)

    @pl.when(me >= MAXLAG)
    def _():
        wait_for(send_r, r_ss)


def on_device(features, block_orders, offsets, tap_gains, weights, signal, block_owner):
    hbm = pl.BlockSpec(memory_space=pltpu.HBM)
    vmem = pl.BlockSpec(memory_space=pltpu.VMEM)
    sem = pltpu.SemaphoreType.DMA
    owner = block_owner.reshape(1, block_owner.shape[1])
    energy, scores = pl.pallas_call(
        kernel,
        out_shape=(
            jax.ShapeDtypeStruct((KC, 1, NT), F32),
            jax.ShapeDtypeStruct((KC, 1, CAP), F32),
        ),
        in_specs=[hbm] * 7,
        out_specs=(vmem, vmem),
        scratch_shapes=[
            pltpu.VMEM((KC - 1, NT), jnp.int32),
            pltpu.SMEM(offsets.shape, jnp.int32),
            pltpu.SMEM(tap_gains.shape, F32),
            pltpu.VMEM(owner.shape, jnp.int32),
            pltpu.VMEM((ROWS, FZ), BF16),
            pltpu.VMEM((ROWS, V), BF16),
            pltpu.VMEM((F, V), BF16),
            pltpu.VMEM((ROWS + 2 * MAXLAG, FZ), F32),
            pltpu.VMEM((NT, FZ // LANES, LANES), F32),
            pltpu.VMEM((NT, FZ // LANES, LANES), F32),
            pltpu.VMEM((NZ, NT, FZ), BF16),
            pltpu.VMEM((NZ, MAXLAG, FZ), BF16),
            pltpu.VMEM((NT, VT, LANES), F32),
            pltpu.VMEM((NT, VT, LANES), BF16),
            pltpu.VMEM((NT, VT, LANES), BF16),
            pltpu.VMEM((KC, NT, V), F32),
            pltpu.VMEM((NT, V), F32),
            pltpu.VMEM((MAXLAG, VT, LANES), F32),
            pltpu.VMEM((NT, VT, LANES), F32),
            pltpu.VMEM((NT, V), BF16),
            pltpu.VMEM(((KC + 1) * V, 2 * LANES), BF16),
            pltpu.VMEM((3 * NT, (KC + 1) * V), BF16),
            pltpu.VMEM((NT, 2, LANES), F32),
            pltpu.VMEM((NT, 2, LANES), F32),
            sem((7,)),
            sem, sem, sem, sem, sem, sem, sem, sem((NZ,)), sem, sem,
            sem, sem,
        ],
        compiler_params=pltpu.CompilerParams(
            collective_id=0, has_side_effects=True, vmem_limit_bytes=58 * 1024 * 1024
        ),
    )(features, block_orders, offsets, tap_gains, weights, signal, owner)
    return jnp.transpose(energy, (1, 2, 0)), jnp.transpose(scores, (1, 2, 0))


def solution(mesh):
    placed = (
        P("tr", "subj"),
        P(),
        P(),
        P(),
        P("subj", None, None),
        P("subj", "tr", None),
        P("subj", None, None),
    )
    return jax.shard_map(
        on_device,
        mesh=mesh,
        in_specs=placed,
        out_specs=(P("subj", "tr", None), P("subj", "tr", None)),
        check_vma=False,
    )
```

time: 54.9 us -> 44.8 us (0.82)
  local copies, waits for them, and re-layouts: 7.72 us -> 2.49 us
  Pallas kernels: 46.2 us -> 41.5 us
    unnamed x16 -> x2, local copies, waits for them, and re-layouts: 7.72 us -> 2.49 us
    pallas_call x1, Pallas kernels: 46.2 us -> 41.5 us  [on_device(): pl.pallas_call(kernel, out_shape=(jax.ShapeDtypeStruct((KC, 1, NT), F32),...]
where the time goes in v2:
time: 44.8 us; the launch traced here: 44.6 us
  Pallas kernels  41.5 us (93%)
  local copies, waits for them, and re-layouts  2.49 us (6%)
  between operations  0.64 us (1%)
    pallas_call x1, Pallas kernels, on_device(): pl.pallas_call(kernel, out_shape=(jax.ShapeDtypeStruct((KC, 1, NT), F32),...  41.5 us
    unnamed x2, local copies, waits for them, and re-layouts  2.49 us

profile of v2, /device:TPU:1, one launch (start us, length us, event | category | flops | bytes accessed | tf_op | source)
XLA Modules:
  0.0 44.6 jit_solution(17165689093010161241)
XLA Ops:
  0.6 41.5 %shard_map.86 = (f32[5,1,64]{2,1,0:T(1,128)}, f32[5,1,8]{2,1,0:T(1,128)}) custom-call(bf16[64,256]{1,0:T(8,128)(2,1)} %feat_hbm.1, s32[4,64]{1,0:T(4,128)} %orders_hbm.1, s32[4,4]{1,0:T(4,128)} %offs_hbm.1, f32[4,4]{1,0:T(4,128)} %gains_hbm.1, bf16[1,2048,1024]{2,1,0:T(8,128)(2,1)} %w_hbm.1, bf16[1,64,1024]{2,1,0:T(8,128)(2,1)} %sig_hbm.1, s32[1,256]{1,0:T(1,128)} %bitcast.5), custom_call_target="tpu_custom_call" | custom-call | tf_op jit(solution)/shard_map/pallas_call | solution.py:299
  42.1 1.3 %copy.11 = f32[1,64,5]{1,0,2:T(1,128)} copy(f32[1,64,5]{1,0,2:T(1,128)} %bitcast.4) | data formatting | bytes 2560
  43.4 1.2 %copy.12 = f32[1,8,5]{1,0,2:T(1,128)} copy(f32[1,8,5]{1,0,2:T(1,128)} %bitcast.3) | data formatting | bytes 320
